TPU v7x, 32 devices: a whole 2x2x4 slice. The times are simulated.
32 devices in a mesh: slab: 4 (over y, x), brick: 8 (over z, core).
Axes of the slice: x: 2, y: 2, z: 4, core: 2. Of those that a mesh axis runs over, the one named last changes fastest.
Arguments:
- k_coeffs: float32 [8, 16, 16, 128], P('slab', 'brick'), may hold values from -0.3 to 0.4
- v_basis: float32 [32768, 128], P(('slab', 'brick')), may hold values from -4 to 4
Outputs:
- basis_x: float32 [8, 16, 16, 128], P('slab', 'brick')
- coupling: float32 [128, 128], replicated
- basis_v: float32 [32768, 128], P(('slab', 'brick'))
All inputs are finite; a program needn't handle non-finite values.
Results may differ from a plain program's by a relative error of at most 0.0001.
Values sent between devices are 32-bit elements; how exact they have to be, the bound alone decides.
A program may use at most 64 MiB of HBM per device.

v0:
```python
import math
import jax
import jax.numpy as jnp
from jax import lax
from jax.sharding import PartitionSpec as P

NVX = 32
CFL = 0.9
VMAX = 6.0
COLLIDE = 0.3
RHO_MIN = 0.25
TEMP_MIN = 0.25
PRECISE = lax.Precision.HIGHEST


def with_halo(array, sides, width):
    for axis, dim in sides:
        peers, length = (lax.axis_size(axis), array.shape[dim])
        up = [(i, (i + 1) % peers) for i in range(peers)]
        down = [(j, i) for i, j in up]
        last = lax.slice_in_dim(array, length - width, length, axis=dim)
        leading = lax.slice_in_dim(array, 0, width, axis=dim)
        before = lax.ppermute(last, axis, up)
        after = lax.ppermute(leading, axis, down)
        array = jnp.concatenate([before, array, after], axis=dim)
    return array


def velocities(indices):
    spacing = 2.0 * VMAX / NVX
    first_index = indices // (NVX * NVX)
    second = indices // NVX % NVX
    third_index = indices % NVX
    coords = jnp.stack([first_index, second, third_index]).astype(jnp.float32)
    return -VMAX + (coords + 0.5) * spacing


def maxwell(cell_params, velocity):
    distance = (velocity[0][None, :] - cell_params[1][:, None]) ** 2
    distance = distance + (velocity[1][None, :] - cell_params[2][:, None]) ** 2
    distance = distance + (velocity[2][None, :] - cell_params[3][:, None]) ** 2
    amplitude = cell_params[0] * (2.0 * math.pi * cell_params[4]) ** (-1.5)
    return amplitude[:, None] * jnp.exp(distance * (-0.5 / cell_params[4])[:, None])


def cell_state(vectors, coeffs):
    moments = lax.dot_general(vectors, coeffs, (((1,), (1,)), ((), ())), precision=PRECISE)
    density = jnp.maximum(moments[0], RHO_MIN)
    drift_speed = moments[1:4] / density[None, :]
    temper = jnp.maximum(
        (moments[4] / density - jnp.sum(drift_speed * drift_speed, axis=0)) / 3.0, TEMP_MIN
    )
    return jnp.concatenate([density[None], drift_speed, temper[None]], axis=0)


def transport_flux(backward, forward, transport):
    flux = jnp.zeros_like(backward[0])
    for axis_id in range(3):
        flux = flux + jnp.dot(backward[axis_id], transport[axis_id], precision=PRECISE)
        flux = flux + jnp.dot(forward[axis_id], transport[3 + axis_id], precision=PRECISE)
    return flux


def products(left_side, backward, forward, maxwell_proj):
    pieces = [
        lax.dot_general(left_side, item, (((0,), (0,)), ((), ())), precision=PRECISE)
        for item in backward + forward + [maxwell_proj]
    ]
    return jnp.stack(pieces)


def coupling_step(coupling_hat, minus_side, plus_side, projected, transport, time_step):
    drift_sum = jnp.zeros_like(coupling_hat)
    for axis_id in range(3):
        drift_sum = drift_sum + jnp.dot(
            jnp.dot(minus_side[axis_id], coupling_hat, precision=PRECISE),
            transport[axis_id],
            precision=PRECISE,
        )
        drift_sum = drift_sum + jnp.dot(
            jnp.dot(plus_side[axis_id], coupling_hat, precision=PRECISE),
            transport[3 + axis_id],
            precision=PRECISE,
        )
    return coupling_hat + time_step * drift_sum - COLLIDE * (projected - coupling_hat)


def velocity_step(velocity_part, minus_side, plus_side, back_proj, positive, negative, time_step):
    drift_sum = jnp.zeros_like(velocity_part)
    for axis_id in range(3):
        drift_sum = drift_sum + positive[axis_id][:, None] * jnp.dot(
            velocity_part, minus_side[axis_id].T, precision=PRECISE
        )
        drift_sum = drift_sum + negative[axis_id][:, None] * jnp.dot(
            velocity_part, plus_side[axis_id].T, precision=PRECISE
        )
    return velocity_part - time_step * drift_sum + COLLIDE * (back_proj - velocity_part)


def slopes(padded, lengths):
    rank_size = padded.shape[3]
    centre = padded[1:-1, 1:-1]
    backward = [
        (centre - padded[:-2, 1:-1]) * lengths[0],
        (centre - padded[1:-1, :-2]) * lengths[1],
        (centre - jnp.roll(centre, 1, axis=2)) * lengths[2],
    ]
    forward = [
        (padded[2:, 1:-1] - centre) * lengths[0],
        (padded[1:-1, 2:] - centre) * lengths[1],
        (jnp.roll(centre, -1, axis=2) - centre) * lengths[2],
    ]
    return (
        [item.reshape(-1, rank_size) for item in backward],
        [item.reshape(-1, rank_size) for item in forward],
    )


def local(k_coeffs, v_basis):
    cells_x, cells_y, cells_z, rank_size = k_coeffs.shape
    cell_count = cells_x * cells_y * cells_z
    slab_count = lax.axis_size("slab")
    brick_count = lax.axis_size("brick")
    devices = slab_count * brick_count
    lengths = (cells_x * slab_count, cells_y * brick_count, cells_z)
    time_step = CFL / (VMAX * (lengths[0] + lengths[1] + lengths[2]))
    weight_x = 1.0 / (lengths[0] * lengths[1] * lengths[2])
    weight_v = (2.0 * VMAX / NVX) ** 3
    row_count = v_basis.shape[0]
    device = lax.axis_index("slab") * brick_count + lax.axis_index("brick")
    row_ids = device * row_count + jnp.arange(row_count, dtype=jnp.int32)
    velocity = velocities(row_ids)
    positive = jnp.maximum(velocity, 0.0)
    negative = jnp.minimum(velocity, 0.0)
    weights = jnp.stack(
        [
            jnp.ones_like(velocity[0]),
            velocity[0],
            velocity[1],
            velocity[2],
            jnp.sum(velocity * velocity, axis=0),
        ]
    )
    vectors = jnp.dot(weights, v_basis, precision=PRECISE) * weight_v
    transport = jnp.stack(
        [
            lax.dot_general(
                v_basis * (side[axis_id] * weight_v)[:, None],
                v_basis,
                (((0,), (0,)), ((), ())),
                precision=PRECISE,
            )
            for side in (positive, negative)
            for axis_id in range(3)
        ]
    )
    transport, vectors = lax.psum((transport, vectors), ("slab", "brick"))
    coeff_flat = k_coeffs.reshape(cell_count, rank_size)
    cell_params = cell_state(vectors, coeff_flat)
    params_all = lax.all_gather(cell_params, ("slab", "brick"), axis=1, tiled=True)
    row_total = cell_count * devices
    block_rows = math.gcd(row_total, 512)

    def one_block(turn_index):
        part_params = lax.dynamic_slice_in_dim(
            params_all, 0 + turn_index * block_rows, block_rows, 1
        )
        return jnp.dot(maxwell(part_params, velocity), v_basis, precision=PRECISE) * weight_v

    blocks = lax.map(one_block, jnp.arange(row_total // block_rows, dtype=jnp.int32))
    whole_term = lax.psum(blocks.reshape(row_total, rank_size), ("slab", "brick"))
    maxwell_proj = lax.dynamic_slice_in_dim(whole_term, device * cell_count, cell_count, 0)
    padded = with_halo(k_coeffs, (("slab", 0), ("brick", 1)), 1)
    backward, forward = slopes(padded, lengths)
    advanced = (
        coeff_flat
        - time_step * transport_flux(backward, forward, transport)
        + COLLIDE * (maxwell_proj - coeff_flat)
    )
    identity = jnp.eye(rank_size, dtype=jnp.float32)
    padded_new = with_halo(
        advanced.reshape(cells_x, cells_y, cells_z, rank_size), (("slab", 0), ("brick", 1)), 1
    )
    backward, forward = slopes(padded_new, lengths)
    local_sums = jnp.concatenate(
        [
            lax.dot_general(advanced, advanced, (((0,), (0,)), ((), ())), precision=PRECISE)[None],
            products(advanced, backward, forward, maxwell_proj),
        ],
        axis=0,
    )
    reduced_all = lax.psum(local_sums * weight_x, ("slab", "brick"))
    factor = jnp.linalg.cholesky(reduced_all[0])
    inverse = jax.scipy.linalg.solve_triangular(factor, identity, lower=True)
    basis_new = jnp.dot(advanced, inverse.T, precision=PRECISE)
    mapped = jnp.einsum("ab,kbc,dc->kad", inverse, reduced_all[1:7], inverse, precision=PRECISE)
    minus_side = mapped[0:3]
    plus_side = mapped[3:6]
    projected = jnp.dot(inverse, reduced_all[7], precision=PRECISE)
    coupling_mid = coupling_step(factor.T, minus_side, plus_side, projected, transport, time_step)
    rows_piece = lax.all_gather(basis_new, ("slab", "brick"), axis=0, tiled=True)
    piece_rows = rows_piece.shape[0]
    fold_block_rows = math.gcd(piece_rows, 512)

    def add_block(turn_index, accumulated):
        offset = turn_index * fold_block_rows
        part_params = lax.dynamic_slice_in_dim(params_all, offset, fold_block_rows, 1)
        basis_block = lax.dynamic_slice_in_dim(rows_piece, offset, fold_block_rows, 0)
        values = maxwell(part_params, velocity)
        return (
            accumulated
            + lax.dot_general(values, basis_block, (((0,), (0,)), ((), ())), precision=PRECISE)
            * weight_x
        )

    back_proj = lax.fori_loop(
        0, piece_rows // fold_block_rows, add_block, jnp.zeros((row_count, rank_size), jnp.float32)
    )
    velocity_part = jnp.dot(v_basis, coupling_mid.T, precision=PRECISE)
    velocity_new = velocity_step(
        velocity_part, minus_side, plus_side, back_proj, positive, negative, time_step
    )
    gram_v = (
        lax.dot_general(velocity_new, velocity_new, (((0,), (0,)), ((), ())), precision=PRECISE)
        * weight_v
    )
    gram_v = lax.psum(gram_v, ("slab", "brick"))
    coupling = jnp.linalg.cholesky(gram_v)
    inverse_v = jax.scipy.linalg.solve_triangular(coupling, identity, lower=True)
    vbasis_new = jnp.dot(velocity_new, inverse_v.T, precision=PRECISE)
    return (basis_new.reshape(cells_x, cells_y, cells_z, rank_size), coupling, vbasis_new)


def solution(mesh):
    placed = (P("slab", "brick", None, None), P(("slab", "brick"), None))
    return jax.shard_map(
        local,
        mesh=mesh,
        in_specs=placed,
        out_specs=(P("slab", "brick", None, None), P(), P(("slab", "brick"), None)),
        check_vma=False,
    )
```

profile of v0, /device:TPU:1, one launch (start us, length us, event | category | flops | bytes accessed | tf_op | source)
XLA Modules:
  0.0 666.3 jit_solution(5660774620069274221)
XLA Ops:
  8.0 2.0 collective-permute-start
  12.6 39.6 %psum.36 = f32[5,128]{1,0:T(8,128)S(1)} all-reduce(f32[5,128]{1,0:T(8,128)S(1)} %convolution_multiply_fusion.7), channel_id=1, replica_groups=mesh['slab'=4,'brick'=8] {'slab','brick'}, use_global_device_ids=true, to_apply=%region_2.3 | all-reduce | flops 640 | bytes 5120 | tf_op jit(solution)/shard_map/psum | solution.py:157
  53.1 43.0 %all-gather = f32[32,64,5]{1,2,0:T(8,128)S(1)} all-gather(f32[1,64,5]{1,2,0:T(8,128)S(1)} %maximum_bitcast_fusion), channel_id=1, replica_groups=mesh['slab'=4,'brick'=8] {'slab','brick'}, dimensions={0}, use_global_device_ids=true | all-gather | bytes 42240 | tf_op jit(solution)/shard_map/all_gather | solution.py:160
  96.2 18.5 %while.24 = (s32[]{:T(128)}, f32[4,512,128]{2,1,0:T(8,128)}, s32[4]{0:T(128)S(1)}, f32[5,2048]{1,0:T(8,128)S(1)}, f32[3,1024]{1,0:T(4,128)S(1)}, /*index=5*/f32[...) while((s32[]{:T(128)}, f32[4,512,128]{2,1,0:T(8,128)}, ...), condition=%wide.region_5.6_spmd, body=%wide.region_4.5_spmd.sunk | while | flops 810616320 | bytes 854787 | solution.py:170
  97.6 3.3 fusion.244
  102.2 3.3 fusion.244
  106.8 3.3 fusion.244
  111.5 3.3 fusion.244
  124.0 3.9 collective-permute-done.3
  128.0 122.3 %all-reduce.9.cloned.1.call-done = (f32[6,128,128]{2,1,0:T(8,128)}, f32[2048,128]{1,0:T(8,128)}) async-done(((f32[6,128,128]{2,1,0:T(8,128)}, f32[2048,128]{1,0:T(8,128)}), (f32[6,128,128]{2,1,0:T(8,128)}, f32[2048,128]{1,0:T(8,128)})) %all-reduce.9.cloned.1.call-update) | async-done | bytes 1441808 | tf_op jit(solution)/shard_map/psum | solution.py:157
  260.4 4.1 collective-permute-start.6
  265.6 2.7 collective-permute-done.7
  272.1 129.2 %all-reduce.5.cloned.1.call-done = f32[8,128,128]{1,2,0:T(8,128)} async-done(((f32[8,128,128]{1,2,0:T(8,128)}), f32[8,128,128]{1,2,0:T(8,128)}) %all-reduce.5.cloned.1.call-update) | async-done | bytes 524304 | tf_op jit(solution)/shard_map/psum | solution.py:192
  403.2 11.7 %cholesky.44 = f32[128,128]{1,0:T(8,128)S(1)} custom-call(f32[128,128]{1,0:T(8,128)S(1)} %fusion.103), custom_call_target="Cholesky" | custom-call | tf_op jit(solution)/shard_map/jit(cholesky)/cholesky | solution.py:193
  416.2 9.8 %custom-call.7 = f32[1,128,128]{1,2,0:T(8,128)S(1)} custom-call(f32[1,128,128]{2,1,0:T(8,128)S(1)} %select_bitcast_fusion.1), custom_call_target="InvertDiagBlocksLowerTriangular" | custom-call | tf_op jit(solution)/shard_map/jit(_solve_triangular)/triangular_solve | solution.py:194
  441.0 47.2 %all-gather.3.cloned.1.call-done = f32[2048,128]{1,0:T(8,128)} async-done(((f32[64,128]{1,0:T(8,128)}), f32[2048,128]{1,0:T(8,128)}) %all-gather.3.cloned.1.call-update) | async-done | bytes 1048592 | tf_op jit(solution)/shard_map/all_gather | solution.py:201
  488.2 21.7 %while.25 = (s32[]{:T(128)}, f32[1024,128]{1,0:T(8,128)S(1)}, f32[5,2048]{1,0:T(8,128)S(1)}, f32[3,1024]{1,0:T(4,128)S(1)}, f32[2048,128]{1,0:T(8,128)}, /*index...) while((s32[]{:T(128)}, f32[1024,128]{1,0:T(8,128)S(1)}, ...), condition=%wide.region_11.14_spmd.clone, body=%wide.region_10.13_spmd.clone.sunk | while | flops 810944000 | bytes 1378557 | solution.py:216
  488.3 5.2 fusion.248
  493.7 5.2 fusion.248
  499.1 5.2 fusion.248
  504.5 5.2 fusion.248
  512.1 120.0 %all-reduce.7.cloned.1.call-done = f32[128,128]{0,1:T(8,128)} async-done(((f32[128,128]{0,1:T(8,128)}), f32[128,128]{0,1:T(8,128)}) %all-reduce.7.cloned.1.call-update) | async-done | bytes 65552 | tf_op jit(solution)/shard_map/psum | solution.py:227
  633.9 11.7 %cholesky.55 = f32[128,128]{1,0:T(8,128)S(1)} custom-call(f32[128,128]{1,0:T(8,128)S(1)} %fusion.105), custom_call_target="Cholesky" | custom-call | tf_op jit(solution)/shard_map/jit(cholesky)/cholesky | solution.py:228
  647.6 9.8 %custom-call.8 = f32[1,128,128]{1,2,0:T(8,128)S(1)} custom-call(f32[1,128,128]{2,1,0:T(8,128)S(1)} %get-tuple-element.175), custom_call_target="InvertDiagBlocksLowerTriangular" | custom-call | tf_op jit(solution)/shard_map/jit(_solve_triangular)/triangular_solve | solution.py:229
  (150 shorter events, 57.4 us)
Async XLA Ops:
  7.2 89.0 %copy-start = (f32[1024,128]{1,0:T(8,128)S(1)}, f32[1024,128]{1,0:T(8,128)}, u32[]{:S(2)}) copy-start(f32[1024,128]{1,0:T(8,128)} %param.10) | copy-start | bytes 1572868
  7.2 243.2 %all-reduce.9.cloned.1.call-start = ((), (), s32[]{:S(2)}) async-start(), calls=%async_computation.3 | async-start | bytes 2883584 | tf_op jit(solution)/shard_map/psum | solution.py:157
  8.0 114.7 %collective-permute-start = (f32[1,2,16,128]{3,2,1,0:T(8,128)S(1)}, f32[1,2,16,128]{3,2,1,0:T(8,128)S(1)}, u32[]{:S(2)}, u32[]{:S(2)}) collective-permute-start(f32[1,2,16,128]{3,2,1,0:T(8,128)S(1)} %get-tuple-element.222), channel_id=1, source_target_pairs={{0,8},{8,16},{16,24},{24,0},{1,9},{9,17},{17,25},{25,1},{2,10},{10... | collective-permute-start | bytes 49160 | tf_op jit(solution)/shard_map/ppermute | solution.py:23
  10.0 112.7 %collective-permute-start.1 = (f32[1,2,16,128]{3,2,1,0:T(8,128)S(1)}, f32[1,2,16,128]{3,2,1,0:T(8,128)S(1)}, u32[]{:S(2)}, u32[]{:S(2)}) collective-permute-start(f32[1,2,16,128]{3,2,1,0:T(8,128)S(1)} %get-tuple-element.221), channel_id=1, source_target_pairs={{8,0},{16,8},{24,16},{0,24},{9,1},{17,9},{25,17},{1,25},{10,2},{18... | collective-permute-start | bytes 49160 | tf_op jit(solution)/shard_map/ppermute | solution.py:24
  120.7 2.0 copy-start.1
  121.9 0.7 copy-start.4
  122.6 278.7 %all-reduce.5.cloned.1.call-start = ((), (), s32[]{:S(2)}) async-start(), calls=%async_computation | async-start | bytes 1048576 | tf_op jit(solution)/shard_map/psum | solution.py:192
  122.8 1.3 collective-permute-start.2
  122.8 5.1 collective-permute-start.3
  256.6 3.5 collective-permute-start.4
  257.8 2.6 collective-permute-start.5
  260.4 5.1 collective-permute-start.6
  264.5 3.8 collective-permute-start.7
  272.0 216.2 %all-gather.3.cloned.1.call-start = ((), (), s32[]{:S(2)}) async-start(), calls=%async_computation.1 | async-start | bytes 1081344 | tf_op jit(solution)/shard_map/all_gather | solution.py:201
  401.3 25.0 %copy-start.3 = (f32[8,128,128]{1,2,0:T(8,128)S(1)}, f32[8,128,128]{1,2,0:T(8,128)}, u32[]{:S(2)}) copy-start(f32[8,128,128]{1,2,0:T(8,128)} %all-reduce.5.cloned.1.call-done) | copy-start | bytes 1572868
  426.8 6.9 %copy-start.2 = (f32[6,128,128]{2,1,0:T(8,128)S(1)}, f32[6,128,128]{2,1,0:T(8,128)}, u32[]{:S(2)}) copy-start(f32[6,128,128]{2,1,0:T(8,128)} %get-tuple-element.173) | copy-start | bytes 1179652
  434.0 198.1 %all-reduce.7.cloned.1.call-start = ((), (), s32[]{:S(2)}) async-start(), calls=%async_computation.2 | async-start | bytes 131072 | tf_op jit(solution)/shard_map/psum | solution.py:227
Sparse Core Ops, SparseCore 0:
  122.8 127.5 all-reduce.8
  272.1 129.1 all-reduce.4
  434.1 54.0 all-gather.2
  512.3 119.8 all-reduce.6
where the time goes:
time: 676 us; the launch traced here: 666 us
  waiting for transfers between devices  428 us (63%)
  blocking collectives  82.5 us (12%)
  matrix products  71.2 us (11%)
  other arithmetic  49.9 us (7%)
  between operations  14.6 us (2%)
  starting transfers between devices  10.9 us (2%)
    psum x1, waiting for transfers between devices, local(): reduced_all = lax.psum(local_sums * weight_x, ('slab', 'brick'))  129 us
    psum x1, waiting for transfers between devices, local(): transport, vectors = lax.psum((transport, vectors), ('slab', 'brick'))  122 us
    psum x1, waiting for transfers between devices, local(): gram_v = lax.psum(gram_v, ('slab', 'brick'))  120 us
    all_gather x1, waiting for transfers between devices, local(): lax.all_gather(basis_new, ('slab', 'brick'), axis=0, tiled=True)  47.2 us
    all_gather x1, blocking collectives, local(): lax.all_gather(cell_params, ('slab', 'brick'), axis=1, tiled=True)  43 us
    psum x1, blocking collectives, local(): transport, vectors = lax.psum((transport, vectors), ('slab', 'brick'))  39.6 us
    dot_general x4, matrix products, add_block(): lax.dot_general(values, basis_block, (((0,), (0,)), ((), ())), precision=...  21 us
  transfers between devices with their start and end apart: 12, of which 10 were waited for; matrix products, arithmetic and copies ran while one was open for 5% of the time, Pallas kernels for 0%

commit v1 on v0

--- a/solution.py
+++ b/solution.py
@@ -224,7 +224,8 @@
         lax.dot_general(velocity_new, velocity_new, (((0,), (0,)), ((), ())), precision=PRECISE)
         * weight_v
     )
-    gram_v = lax.psum(gram_v, ("slab", "brick"))
+    shards = lax.all_gather(gram_v, ("slab", "brick"))
+    gram_v = jnp.sum(shards, axis=0)
     coupling = jnp.linalg.cholesky(gram_v)
     inverse_v = jax.scipy.linalg.solve_triangular(coupling, identity, lower=True)
     vbasis_new = jnp.dot(velocity_new, inverse_v.T, precision=PRECISE)

time: 676 us -> 619 us (0.916)
  waiting for transfers between devices: 428 us -> 363 us
  matrix products: 71.2 us -> 79.8 us
    psum x1 -> x0, waiting for transfers between devices: 120 us -> none  [local(): gram_v = lax.psum(gram_v, ('slab', 'brick'))]
    all_gather x0 -> x1, waiting for transfers between devices: none -> 55.5 us  [local(): shards = lax.all_gather(gram_v, ('slab', 'brick'))]
  transfers between devices with their start and end apart: 12 -> 12, of which waited for: 10 -> 10; matrix products, arithmetic and copies ran while one was open for 5% -> 7% of each run, Pallas kernels for 0% -> 0%
where the time goes in v1:
time: 619 us; the launch traced here: 609 us
  waiting for transfers between devices  363 us (59%)
  blocking collectives  82.5 us (13%)
  matrix products  79.8 us (13%)
  other arithmetic  50.8 us (8%)
  between operations  14.6 us (2%)
  starting transfers between devices  10.9 us (2%)
    psum x1, waiting for transfers between devices, local(): reduced_all = lax.psum(local_sums * weight_x, ('slab', 'brick'))  129 us
    psum x1, waiting for transfers between devices, local(): transport, vectors = lax.psum((transport, vectors), ('slab', 'brick'))  122 us
    all_gather x1, waiting for transfers between devices, local(): shards = lax.all_gather(gram_v, ('slab', 'brick'))  55.5 us
    all_gather x1, waiting for transfers between devices, local(): lax.all_gather(basis_new, ('slab', 'brick'), axis=0, tiled=True)  46.3 us
    all_gather x1, blocking collectives, local(): lax.all_gather(cell_params, ('slab', 'brick'), axis=1, tiled=True)  43 us
    psum x1, blocking collectives, local(): transport, vectors = lax.psum((transport, vectors), ('slab', 'brick'))  39.6 us
    dot_general x4, matrix products, add_block(): lax.dot_general(values, basis_block, (((0,), (0,)), ((), ())), precision=...  21 us
    dot_general x4, matrix products, one_block(): jnp.dot(maxwell(part_params, velocity), v_basis, precision=PRECISE)  17.3 us
  transfers between devices with their start and end apart: 12, of which 10 were waited for; matrix products, arithmetic and copies ran while one was open for 7% of the time, Pallas kernels for 0%

profile of v1, /device:TPU:1, one launch (start us, length us, event | category | flops | bytes accessed | tf_op | source)
XLA Modules:
  0.0 609.4 jit_solution(7442161873554444593)
XLA Ops:
  12.5 39.6 %psum.29 = f32[5,128]{1,0:T(8,128)S(1)} all-reduce(f32[5,128]{1,0:T(8,128)S(1)} %convolution_multiply_fusion.7), channel_id=1, replica_groups=mesh['slab'=4,'brick'=8] {'slab','brick'}, use_global_device_ids=true, to_apply=%region_2.3 | all-reduce | flops 640 | bytes 5120 | tf_op jit(solution)/shard_map/psum | solution.py:157
  53.1 43.0 %all-gather.1 = f32[32,64,5]{1,2,0:T(8,128)S(1)} all-gather(f32[1,64,5]{1,2,0:T(8,128)S(1)} %maximum_bitcast_fusion), channel_id=1, replica_groups=mesh['slab'=4,'brick'=8] {'slab','brick'}, dimensions={0}, use_global_device_ids=true | all-gather | bytes 42240 | tf_op jit(solution)/shard_map/all_gather | solution.py:160
  96.1 22.7 %while.24 = (s32[]{:T(128)}, f32[4,512,128]{2,1,0:T(8,128)}, s32[4]{0:T(128)S(1)}, f32[5,2048]{1,0:T(8,128)S(1)}, f32[3,1024]{1,0:T(4,128)S(1)}, /*index=5*/f32[...) while((s32[]{:T(128)}, f32[4,512,128]{2,1,0:T(8,128)}, ...), condition=%wide.region_5.6_spmd, body=%wide.region_4.5_spmd.sunk | while | flops 810616320 | bytes 854787 | solution.py:170
  97.5 4.3 fusion.244
  103.2 4.3 fusion.244
  108.9 4.3 fusion.244
  114.5 4.3 fusion.244
  118.9 2.4 fusion.82
  130.7 3.9 collective-permute-done.3
  134.7 122.4 %all-reduce.6.cloned.1.call-done = (f32[6,128,128]{2,1,0:T(8,128)}, f32[2048,128]{1,0:T(8,128)}) async-done(((f32[6,128,128]{2,1,0:T(8,128)}, f32[2048,128]{1,0:T(8,128)}), (f32[6,128,128]{2,1,0:T(8,128)}, f32[2048,128]{1,0:T(8,128)})) %all-reduce.6.cloned.1.call-update) | async-done | bytes 1441808 | tf_op jit(solution)/shard_map/psum | solution.py:157
  267.1 4.1 collective-permute-start.6
  272.3 2.7 collective-permute-done.7
  278.8 129.2 %all-reduce.4.cloned.1.call-done = f32[8,128,128]{1,2,0:T(8,128)} async-done(((f32[8,128,128]{1,2,0:T(8,128)}), f32[8,128,128]{1,2,0:T(8,128)}) %all-reduce.4.cloned.1.call-update) | async-done | bytes 524304 | tf_op jit(solution)/shard_map/psum | solution.py:192
  409.8 11.7 %cholesky.44 = f32[128,128]{1,0:T(8,128)S(1)} custom-call(f32[128,128]{1,0:T(8,128)S(1)} %fusion.103), custom_call_target="Cholesky" | custom-call | tf_op jit(solution)/shard_map/jit(cholesky)/cholesky | solution.py:193
  422.9 9.8 %custom-call.7 = f32[1,128,128]{1,2,0:T(8,128)S(1)} custom-call(f32[1,128,128]{2,1,0:T(8,128)S(1)} %select_bitcast_fusion.1), custom_call_target="InvertDiagBlocksLowerTriangular" | custom-call | tf_op jit(solution)/shard_map/jit(_solve_triangular)/triangular_solve | solution.py:194
  449.5 46.3 %all-gather.5.cloned.1.call-done = f32[2048,128]{1,0:T(8,128)} async-done(((f32[64,128]{1,0:T(8,128)}), f32[2048,128]{1,0:T(8,128)}) %all-gather.5.cloned.1.call-update) | async-done | bytes 1048592 | tf_op jit(solution)/shard_map/all_gather | solution.py:201
  495.9 21.7 %while.25 = (s32[]{:T(128)}, f32[1024,128]{1,0:T(8,128)S(1)}, f32[5,2048]{1,0:T(8,128)S(1)}, f32[3,1024]{1,0:T(4,128)S(1)}, f32[2048,128]{1,0:T(8,128)}, /*index...) while((s32[]{:T(128)}, f32[1024,128]{1,0:T(8,128)S(1)}, ...), condition=%wide.region_11.14_spmd.clone, body=%wide.region_10.13_spmd.clone.sunk | while | flops 810944000 | bytes 1378557 | solution.py:216
  496.0 5.2 fusion.248
  501.4 5.2 fusion.248
  506.7 5.2 fusion.248
  512.1 5.2 fusion.248
  519.8 55.5 %all-gather.7.cloned.1.call-done = f32[4096,128]{1,0:T(8,128)} async-done(((f32[128,128]{1,0:T(8,128)}), f32[4096,128]{1,0:T(8,128)}) %all-gather.7.cloned.1.call-update) | async-done | bytes 2097168 | tf_op jit(solution)/shard_map/all_gather | solution.py:227
  577.1 11.7 %cholesky.55 = f32[128,128]{1,0:T(8,128)S(1)} custom-call(f32[128,128]{1,0:T(8,128)S(1)} %fusion.105), custom_call_target="Cholesky" | custom-call | tf_op jit(solution)/shard_map/jit(cholesky)/cholesky | solution.py:229
  590.8 9.8 %custom-call.8 = f32[1,128,128]{1,2,0:T(8,128)S(1)} custom-call(f32[1,128,128]{2,1,0:T(8,128)S(1)} %get-tuple-element.175), custom_call_target="InvertDiagBlocksLowerTriangular" | custom-call | tf_op jit(solution)/shard_map/jit(_solve_triangular)/triangular_solve | solution.py:230
  (149 shorter events, 61.3 us)
Async XLA Ops:
  7.2 249.9 %all-reduce.6.cloned.1.call-start = ((), (), s32[]{:S(2)}) async-start(), calls=%async_computation.3 | async-start | bytes 2883584 | tf_op jit(solution)/shard_map/psum | solution.py:157
  7.9 121.4 %collective-permute-start = (f32[1,2,16,128]{3,2,1,0:T(8,128)S(1)}, f32[1,2,16,128]{3,2,1,0:T(8,128)S(1)}, u32[]{:S(2)}, u32[]{:S(2)}) collective-permute-start(f32[1,2,16,128]{3,2,1,0:T(8,128)S(1)} %get-tuple-element.222), channel_id=1, source_target_pairs={{0,8},{8,16},{16,24},{24,0},{1,9},{9,17},{17,25},{25,1},{2,10},{10... | collective-permute-start | bytes 49160 | tf_op jit(solution)/shard_map/ppermute | solution.py:23
  10.0 119.4 %collective-permute-start.1 = (f32[1,2,16,128]{3,2,1,0:T(8,128)S(1)}, f32[1,2,16,128]{3,2,1,0:T(8,128)S(1)}, u32[]{:S(2)}, u32[]{:S(2)}) collective-permute-start(f32[1,2,16,128]{3,2,1,0:T(8,128)S(1)} %get-tuple-element.221), channel_id=1, source_target_pairs={{8,0},{16,8},{24,16},{0,24},{9,1},{17,9},{25,17},{1,25},{10,2},{18... | collective-permute-start | bytes 49160 | tf_op jit(solution)/shard_map/ppermute | solution.py:24
  118.9 4.9 copy-start
  126.2 3.2 copy-start.1
  128.5 0.7 copy-start.3
  129.3 278.7 %all-reduce.4.cloned.1.call-start = ((), (), s32[]{:S(2)}) async-start(), calls=%async_computation | async-start | bytes 1048576 | tf_op jit(solution)/shard_map/psum | solution.py:192
  129.5 1.3 collective-permute-start.2
  129.5 5.1 collective-permute-start.3
  263.3 3.5 collective-permute-start.4
  264.5 2.6 collective-permute-start.5
  267.1 5.1 collective-permute-start.6
  271.2 3.8 collective-permute-start.7
  278.7 162.6 %copy-start.2 = (f32[6,128,128]{2,1,0:T(8,128)S(1)}, f32[6,128,128]{2,1,0:T(8,128)}, u32[]{:S(2)}) copy-start(f32[6,128,128]{2,1,0:T(8,128)} %get-tuple-element.173) | copy-start | bytes 1179652
  278.7 217.1 %all-gather.5.cloned.1.call-start = ((), (), s32[]{:S(2)}) async-start(), calls=%async_computation.1 | async-start | bytes 1081344 | tf_op jit(solution)/shard_map/all_gather | solution.py:201
  441.6 133.6 %all-gather.7.cloned.1.call-start = ((), (), s32[]{:S(2)}) async-start(), calls=%async_computation.2 | async-start | bytes 2162688 | tf_op jit(solution)/shard_map/all_gather | solution.py:227
Sparse Core Ops, SparseCore 0:
  129.4 127.5 all-reduce.5
  278.8 129.1 all-reduce.3
  441.8 54.0 all-gather.4
  519.9 55.3 all-gather.6
